TPU v7x, 128 devices: a whole 4x4x4 slice. The times are simulated.
128 devices in a mesh: dp: 4 (over y), fsdp: 4 (over x_lo, core), ctx: 8 (over z, x_hi).
Axes of the slice: x: 4 (x_hi: 2, x_lo: 2; x = x_hi * 2 + x_lo), y: 4, z: 4, core: 2. Of those that a mesh axis runs over, the one named last changes fastest.
Arguments:
- tokens: bfloat16 [16, 4096, 1024], P(('dp', 'fsdp'), 'ctx')
- bounds: int32 [16, 4096], P(('dp', 'fsdp'), 'ctx'), may hold values 0 or 1
- decay_rates: float32 [16], replicated, may hold values from 2.4414063e-05 to 0.9
- w_query: bfloat16 [1024, 1024], P('fsdp')
- w_key: bfloat16 [1024, 1024], P('fsdp')
- w_up: bfloat16 [1024, 2048], P('fsdp'), may hold values from -0.1875 to 0.1875
- grad_out: bfloat16 [16, 4096, 2048], P(('dp', 'fsdp'), 'ctx'), may hold values from -6 to 6
Outputs:
- dechunked: bfloat16 [16, 4096, 2048], P(('dp', 'fsdp'), 'ctx')
- grad_tokens: bfloat16 [16, 4096, 1024], P(('dp', 'fsdp'), 'ctx')
- grad_query: float32 [1024, 1024], P('fsdp')
- grad_key: float32 [1024, 1024], P('fsdp')
- grad_up: float32 [1024, 2048], P('fsdp')
All inputs are finite; a program needn't handle non-finite values. No bound on the sum of `bounds` on one device may be relied on, other than what follows from the above.
Results may differ from a plain program's by a relative error of at most 0.0049.
Values may be sent and summed in bfloat16 or wider, within the bound.
No kernel may reach another device: no remote copies, remote signals or barrier semaphores. Data moves between devices by JAX's collectives and lax.ppermute only.
A program may use at most 128 MiB of HBM per device.

v0:
```python
import jax
import jax.numpy as jnp
from jax import lax
from jax.sharding import PartitionSpec as P

SPAN = 128
epsilon = 1e-06


def shifted(x, axis, by):
    devices = lax.axis_size(axis)
    pairs = [(i, i + by) for i in range(devices) if 0 <= i + by < devices]
    return lax.ppermute(x, axis, pairs)


def carried_in(part, axis, combine, identity, reverse):
    count = lax.axis_size(axis)
    place = lax.axis_index(axis)
    ahead = count - 1 - place if reverse else place
    gathered = jax.tree.map(lambda a: lax.all_gather(a, axis), part)
    state = jax.tree.map(lambda a, e: jnp.zeros_like(a) + jnp.asarray(e, a.dtype), part, identity)

    def one(turn, state):
        source = count - 1 - turn if reverse else turn
        return combine(
            state, jax.tree.map(lambda a: lax.dynamic_index_in_dim(a, source, 0, False), gathered)
        )

    return lax.fori_loop(0, ahead, one, state)


def chain_pair(earlier, latter):
    decay_first, state_first = earlier
    decay_second, state_second = latter
    return (decay_first * decay_second, decay_second[..., None] * state_first + state_second)


def per_device(tokens, bounds, decay_rates, w_query, w_key, w_up, grad_out):
    batch_local, length, model_width = tokens.shape
    hidden = w_up.shape[1]
    head_count = decay_rates.shape[0]
    channels = hidden // head_count
    blocks = length // SPAN
    columns_all = 2 * model_width + hidden
    flat_tokens = tokens.reshape(batch_local * length, model_width)
    panels = jnp.concatenate([w_query, w_key, w_up], 1)
    full_panels = lax.all_gather(panels, "fsdp", axis=0, tiled=True)
    projected = jnp.dot(flat_tokens, full_panels, preferred_element_type=jnp.float32)
    queries = projected[:, :model_width].reshape(batch_local, length, model_width)
    keys_now = projected[:, model_width : 2 * model_width].reshape(batch_local, length, model_width)
    values = projected[:, 2 * model_width :].reshape(
        batch_local, blocks, SPAN, head_count, channels
    )
    key_before = shifted(keys_now[:, -1:, :], "ctx", 1)
    keys_prev = jnp.concatenate([key_before, keys_now[:, :-1]], 1)
    inv_query = lax.rsqrt(jnp.sum(queries * queries, -1) + epsilon)
    inv_key = lax.rsqrt(jnp.sum(keys_prev * keys_prev, -1) + epsilon)
    cosine = jnp.sum(queries * keys_prev, -1) * inv_query * inv_key
    own_index = lax.axis_index("ctx")
    opening = jnp.logical_and(own_index == 0, jnp.arange(length) == 0)[None, :]
    boundary_prob = jnp.where(opening, 1.0, 0.5 * (1.0 - cosine))
    marked = jnp.where(opening, 1.0, bounds.astype(jnp.float32))
    mix_rate = (marked * boundary_prob)[..., None] * decay_rates
    rate_blocks = mix_rate.reshape(batch_local, blocks, SPAN, head_count)
    log_keep = jnp.cumsum(jnp.log(1.0 - rate_blocks), axis=2)
    keep_heads = jnp.moveaxis(log_keep, 3, 2)
    log_gap = keep_heads[..., :, None] - keep_heads[..., None, :]
    offsets = jnp.arange(SPAN)
    lower_mask = offsets[:, None] >= offsets[None, :]
    upper_mask = offsets[:, None] <= offsets[None, :]
    forward_band = (
        jnp.where(lower_mask, jnp.exp(jnp.where(lower_mask, log_gap, -1e30)), 0.0)
        * jnp.moveaxis(rate_blocks, 3, 2)[..., None, :]
    )
    local_states = jnp.einsum(
        "bnhtu,bnuhc->bnthc", forward_band, values, precision=lax.Precision.HIGHEST
    )
    block_logs = log_keep[:, :, -1]
    block_decay = jnp.exp(block_logs)
    running_logs = jnp.cumsum(block_logs, axis=1)
    decay_before = jnp.exp(running_logs - block_logs)
    decay_after = jnp.exp(running_logs[:, -1:] - running_logs)
    device_decay = jnp.exp(running_logs[:, -1])
    inner_zero = jnp.zeros((batch_local, head_count, channels), jnp.float32)

    def walk_blocks(carried, element):
        decay_now, addition = element
        return (decay_now[..., None] * carried + addition, carried)

    device_state, block_in = lax.scan(
        walk_blocks,
        inner_zero,
        (jnp.moveaxis(block_decay, 1, 0), jnp.moveaxis(local_states[:, :, -1], 1, 0)),
    )
    identity_pair = (jnp.ones_like(device_decay), inner_zero)
    _, state_in = carried_in((device_decay, device_state), "ctx", chain_pair, identity_pair, False)
    block_carry = jnp.moveaxis(block_in, 0, 1) + decay_before[..., None] * state_in[:, None]
    states = local_states + jnp.exp(log_keep)[..., None] * block_carry[:, :, None]
    dechunked = states.reshape(batch_local, length, hidden).astype(jnp.bfloat16)
    state_rows = states.reshape(batch_local, length, head_count, channels)
    states_prev = jnp.concatenate([state_in[:, None], state_rows[:, :-1]], 1)
    cotangent = grad_out.astype(jnp.float32).reshape(
        batch_local, blocks, SPAN, head_count, channels
    )
    backward_band = jnp.where(upper_mask, jnp.exp(jnp.where(upper_mask, -log_gap, -1e30)), 0.0)
    local_adjoint = jnp.einsum(
        "bnhtu,bnuhc->bnthc", backward_band, cotangent, precision=lax.Precision.HIGHEST
    )
    block_heads = (1.0 - rate_blocks[:, :, 0])[..., None] * local_adjoint[:, :, 0]
    device_head, block_out = lax.scan(
        walk_blocks,
        inner_zero,
        (jnp.moveaxis(block_decay, 1, 0), jnp.moveaxis(block_heads, 1, 0)),
        reverse=True,
    )
    _, adjoint_in = carried_in((device_decay, device_head), "ctx", chain_pair, identity_pair, True)
    block_from = jnp.moveaxis(block_out, 0, 1) + decay_after[..., None] * adjoint_in[:, None]
    adjoints = (
        local_adjoint + jnp.exp(log_keep[:, :, -1:] - log_keep)[..., None] * block_from[:, :, None]
    )
    adjoint_rows = adjoints.reshape(batch_local, length, head_count, channels)
    d_values = (
        (mix_rate[..., None] * adjoint_rows)
        .reshape(batch_local, length, hidden)
        .astype(jnp.bfloat16)
    )
    value_rows = values.reshape(batch_local, length, head_count, channels)
    d_rate = jnp.sum(adjoint_rows * (value_rows - states_prev), -1)
    d_prob = jnp.where(opening, 0.0, marked * jnp.sum(d_rate * decay_rates, -1))
    d_cos = -0.5 * d_prob
    pair_scale = inv_query * inv_key
    d_query = (
        d_cos[..., None]
        * (
            keys_prev * pair_scale[..., None]
            - (cosine * inv_query * inv_query)[..., None] * queries
        )
    ).astype(jnp.bfloat16)
    d_prev = d_cos[..., None] * (
        queries * pair_scale[..., None] - (cosine * inv_key * inv_key)[..., None] * keys_prev
    )
    key_after = shifted(d_prev[:, :1, :], "ctx", -1)
    d_key = jnp.concatenate([d_prev[:, 1:], key_after], 1).astype(jnp.bfloat16)
    d_all = jnp.concatenate([d_query, d_key, d_values], 2).reshape(
        batch_local * length, columns_all
    )
    d_flat = lax.dot_general(
        d_all, full_panels, (((1,), (1,)), ((), ())), preferred_element_type=jnp.float32
    )
    grad_tokens = d_flat.reshape(batch_local, length, model_width).astype(jnp.bfloat16)
    grads = lax.dot_general(
        flat_tokens, d_all, (((0,), (0,)), ((), ())), preferred_element_type=jnp.float32
    )
    reduced = lax.psum_scatter(grads, "fsdp", scatter_dimension=0, tiled=True)
    summed = lax.psum(reduced, ("dp", "ctx"))
    return (
        dechunked,
        grad_tokens,
        summed[:, :model_width],
        summed[:, model_width : 2 * model_width],
        summed[:, 2 * model_width :],
    )


def solution(mesh):
    return jax.shard_map(
        per_device,
        mesh=mesh,
        in_specs=(
            P(("dp", "fsdp"), "ctx", None),
            P(("dp", "fsdp"), "ctx"),
            P(),
            P("fsdp", None),
            P("fsdp", None),
            P("fsdp", None),
            P(("dp", "fsdp"), "ctx", None),
        ),
        out_specs=(
            P(("dp", "fsdp"), "ctx", None),
            P(("dp", "fsdp"), "ctx", None),
            P("fsdp", None),
            P("fsdp", None),
            P("fsdp", None),
        ),
        check_vma=False,
    )
```

profile of v0, /device:TPU:0, one launch (start us, length us, event | category | flops | bytes accessed | tf_op | source)
XLA Modules:
  0.0 855.9 jit_solution(13481682281090934830)
XLA Ops:
  7.2 3.2 pad_maximum_fusion.2
  10.5 2.0 copy.154
  12.5 0.6 iota_compare_fusion
  13.1 79.9 %all-gather.4.cloned.1.call-done = bf16[1024,4096]{1,0:T(8,128)(2,1)} async-done(((bf16[256,4096]{1,0:T(8,128)(2,1)}), bf16[1024,4096]{1,0:T(8,128)(2,1)}) %all-gather.4.cloned.1.call-update) | async-done | bytes 8388624 | tf_op jit(solution)/shard_map/all_gather | solution.py:47
  93.1 6.9 convolution_bitcast_fusion.1
  100.7 4.6 collective-permute-start
  105.6 2.9 copy.153
  109.4 0.6 multiply_multiply_fusion.1
  110.2 0.8 copy.129
  111.0 1.2 reduce_window_sum.26
  112.9 0.6 copy-done.16
  113.6 7.8 fusion.21
  121.4 1.9 copy-done.6
  123.4 2.9 while.58
  123.4 0.6 fusion.66
  124.8 0.7 fusion.66
  125.6 0.7 fusion.66
  126.3 34.6 %all-gather = f32[8,16,128]{2,1,0:T(8,128)S(1)} all-gather(f32[1,16,128]{2,1,0:T(8,128)S(1)} %get-tuple-element.266), channel_id=2, replica_groups=mesh['dp'=4,'fsdp'=4,'ctx'=8] {'ctx'}, dimensions={0}, use_global_device_ids=true | all-gather | bytes 73728 | tf_op jit(solution)/shard_map/all_gather | solution.py:20
  161.0 0.7 reduce_window_sum.28
  162.2 22.3 %all_gather.22 = f32[8,1,16]{2,1,0:T(1,128)} all-gather(f32[1,1,16]{2,1,0:T(1,128)S(1)} %get-tuple-element.521), channel_id=1, replica_groups=mesh['dp'=4,'fsdp'=4,'ctx'=8] {'ctx'}, dimensions={0}, use_global_device_ids=true | all-gather | bytes 576 | tf_op jit(solution)/shard_map/all_gather | solution.py:20
  184.5 1.5 fusion.50
  186.1 1.3 fusion.53
  187.4 5.0 fusion.18
  192.4 2.0 copy-done.7
  194.6 2.9 while.59
  194.6 0.7 fusion.67
  195.3 0.7 fusion.67
  196.8 0.6 fusion.67
  197.5 35.0 %all-gather.1 = f32[8,16,128]{2,1,0:T(8,128)S(1)} all-gather(f32[1,16,128]{2,1,0:T(8,128)S(1)} %get-tuple-element.269), channel_id=3, replica_groups=mesh['dp'=4,'fsdp'=4,'ctx'=8] {'ctx'}, dimensions={0}, use_global_device_ids=true | all-gather | bytes 73728 | tf_op jit(solution)/shard_map/all_gather | solution.py:20
  232.5 5.4 while.57
  232.5 0.6 dynamic-slice_bitcast_fusion.5
  233.2 0.7 dynamic-slice_bitcast_fusion.5
  235.3 0.6 dynamic-slice_bitcast_fusion.5
  236.0 0.7 dynamic-slice_bitcast_fusion.5
  238.0 0.8 bitcast_add_fusion.4
  238.8 3.8 fusion.59
  242.6 2.4 copy.143
  245.1 2.2 slice.76
  247.4 2.6 pad_maximum_fusion.1
  250.0 0.8 copy-done.3
  250.9 1.3 copy-done.8
  252.2 3.8 fusion.16
  256.2 2.1 multiply_bitcast_fusion
  258.3 1.0 copy-done.9
  259.2 1.3 collective-permute-start.1
  260.5 4.4 copy.146
  265.0 2.8 mul.510
  267.8 9.8 %multiply_convert_fusion = bf16[1,512,2048]{2,0,1:T(2,128)(2,1)} fusion(f32[1,512,2048]{2,0,1:T(1,128)} %bitcast.151, f32[1,512,2048]{2,0,1:T(1,128)} %bitcast.150), kind=kLoop, calls=%fused_computation.34 | loop fusion | flops 2097152 | bytes 10485760 | tf_op jit(solution)/shard_map/convert_element_type | solution.py:125
  277.6 2.2 fusion.47
  280.1 1.6 copy.147
  281.8 1.6 copy.148
  283.4 9.9 %pad_maximum_fusion = bf16[1,512,4096]{2,0,1:T(2,128)(2,1)S(1)} fusion(bf16[1,512,2048]{2,0,1:T(2,128)(2,1)S(1)} %copy-done.2, bf16[1,512,1024]{2,0,1:T(2,128)(2,1)S(1)} %copy.148, bf16[1,512,1024]{2,0,1:T(2,128)(2,1)S(1)} %copy.147), kind=kLoop, calls=%fused_computation.13 | loop fusion | flops 12582912 | bytes 8388608 | tf_op jit(solution)/shard_map/concatenate | solution.py:144
  293.3 3.2 copy-done.5
  296.6 15.4 %convolution_bitcast_fusion = f32[1024,4096]{0,1:T(8,128)} fusion(bf16[1,512,4096]{2,0,1:T(2,128)(2,1)S(1)} %pad_maximum_fusion, bf16[1,512,1024]{2,1,0:T(8,128)(2,1)S(1)} %copy-done), kind=kOutput, calls=%fused_computation.12 | convolution fusion | flops 4294967296 | bytes 22020096 | tf_op jit(solution)/shard_map/dot_general | solution.py:151
  312.1 146.3 %reduce-scatter.2.cloned.1.call-done = f32[256,4096]{0,1:T(8,128)} async-done(((f32[1024,4096]{0,1:T(8,128)}), f32[256,4096]{0,1:T(8,128)}) %reduce-scatter.2.cloned.1.call-update) | async-done | bytes 4194320 | tf_op jit(solution)/shard_map/reduce_scatter | solution.py:154
  458.4 2.7 copy.137
  461.1 4.4 convert_element_type.52
  465.4 14.2 %fusion.44 = bf16[1,512,1024]{2,1,0:T(8,128)(2,1)} fusion(bf16[1024,4096]{1,0:T(8,128)(2,1)} %all-gather.4.cloned.1.call-done, bf16[1,512,4096]{2,0,1:T(2,128)(2,1)} %copy-done.5), kind=kOutput, calls=%fused_computation.64 | convolution fusion | flops 4295491584 | bytes 13631488 | tf_op jit(solution)/shard_map/dot_general | solution.py:147
  479.7 361.8 %all-reduce.2.cloned.1.call-done = f32[256,4096]{0,1:T(8,128)} async-done(((f32[256,4096]{0,1:T(8,128)}), f32[256,4096]{0,1:T(8,128)}) %all-reduce.2.cloned.1.call-update) | async-done | bytes 4194320 | tf_op jit(solution)/shard_map/psum | solution.py:155
  841.4 1.6 slice-done
  843.0 1.8 copy.151
  844.8 1.7 fusion.60
  846.5 1.3 copy.149
  847.8 1.3 copy.150
  (115 shorter events, 8.7 us)
Async XLA Ops:
  7.2 85.9 %copy-start = (bf16[1,512,1024]{2,1,0:T(8,128)(2,1)S(1)}, bf16[1,512,1024]{2,1,0:T(8,128)(2,1)}, u32[]{:S(2)}) copy-start(bf16[1,512,1024]{2,1,0:T(8,128)(2,1)} %param.15) | copy-start | bytes 3145732
  7.2 3.4 copy-start.11
  7.2 85.9 %all-gather.4.cloned.1.call-start = ((), (), s32[]{:S(2)}) async-start(), calls=%async_computation.1 | async-start | bytes 10485760 | tf_op jit(solution)/shard_map/all_gather | solution.py:47
  10.5 447.9 %reduce-scatter.2.cloned.1.call-start = ((), (), s32[]{:S(2)}) async-start(), calls=%async_computation.2 | async-start | bytes 20971520 | tf_op jit(solution)/shard_map/reduce_scatter | solution.py:154
  100.0 8.6 copy-start.1
  100.7 7.8 collective-permute-start
  108.5 1.6 copy-start.23
  108.5 1.6 copy-start.25
  108.5 1.6 copy-start.14
  110.1 2.8 copy-start.18
  112.9 0.6 copy-start.16
  121.4 1.9 copy-start.6
  161.7 22.8 %copy-start.22 = (f32[1,4,16]{2,1,0:T(4,128)}, f32[1,4,16]{2,1,0:T(4,128)S(1)}, u32[]{:S(2)}) copy-start(f32[1,4,16]{2,1,0:T(4,128)S(1)} %reduce_window_sum.28) | copy-start | bytes 772
  187.4 50.5 %copy-start.13 = (f32[4,128,16]{2,1,0:T(8,128)S(1)}, f32[4,128,16]{2,1,0:T(8,128)}, u32[]{:S(2)}) copy-start(f32[4,128,16]{2,1,0:T(8,128)} %get-tuple-element.508) | copy-start | bytes 98308
  192.4 2.0 copy-start.7
  245.1 2.2 copy-start.12
  247.4 3.5 copy-start.3
  247.4 4.7 copy-start.8
  252.1 3.9 copy-start.26
  252.1 4.0 copy-start.24
  252.1 4.0 copy-start.15
  252.1 4.0 copy-start.17
  252.1 4.0 copy-start.21
  258.3 1.0 copy-start.9
  259.2 22.5 %collective-permute-start.1 = (bf16[1,1,1024]{2,1,0:T(2,128)(2,1)S(1)}, bf16[1,1,1024]{2,1,0:T(2,128)(2,1)S(1)}, u32[]{:S(2)}, u32[]{:S(2)}) collective-permute-start(bf16[1,1,1024]{2,1,0:T(2,128)(2,1)S(1)} %slice.78), channel_id=1, source_target_pairs={{1,0},{2,1},{3,2},{4,3},{5,4},{6,5},{7,6},{9,8},{10,9},{11,10},{12... | collective-permute-start | bytes 6152 | tf_op jit(solution)/shard_map/ppermute | solution.py:13
  260.5 4.4 copy-start.19
  267.8 9.8 %copy-start.20 = (f32[512]{0:T(512)S(1)}, f32[512]{0:T(512)}, u32[]{:S(2)}) copy-start(f32[512]{0:T(512)} %get-tuple-element.511) | copy-start | bytes 6148
  277.6 2.2 copy-start.10
  280.0 3.4 copy-start.2
  293.3 3.2 copy-start.5
  312.0 146.4 %copy-start.4 = (bf16[1,4,128,16,128]{4,2,3,1,0:T(8,128)(2,1)S(1)}, bf16[1,4,128,16,128]{4,2,3,1,0:T(8,128)(2,1)}, u32[]{:S(2)}) copy-start(bf16[1,4,128,16,128]{4,2,3,1,0:T(8,128)(2,1)} %get-tuple-element.501) | copy-start | bytes 6291460
  312.0 529.4 %all-reduce.2.cloned.1.call-start = ((), (), s32[]{:S(2)}) async-start(), calls=%async_computation.3 | async-start | bytes 8388608 | tf_op jit(solution)/shard_map/psum | solution.py:155
  841.4 1.6 slice-start
Sparse Core Ops, SparseCore 0:
  10.6 82.4 all-gather.3
  312.1 146.1 reduce-scatter.1
  460.9 380.5 all-reduce.1
where the time goes:
time: 864 us; the launch traced here: 856 us
  waiting for transfers between devices  588 us (68%)
  blocking collectives  92 us (11%)
  local copies, waits for them, and re-layouts  58.6 us (7%)
  matrix products  49.4 us (6%)
  other arithmetic  46.9 us (5%)
  between operations  14.5 us (2%)
    psum x1, waiting for transfers between devices, per_device(): summed = lax.psum(reduced, ('dp', 'ctx'))  362 us
    reduce_scatter x1, waiting for transfers between devices, per_device(): reduced = lax.psum_scatter(grads, 'fsdp', scatter_dimension=0, tiled=True)  146 us
    all_gather x3, blocking collectives, carried_in(): gathered = jax.tree.map(lambda a: lax.all_gather(a, axis), part)  92 us
    all_gather x1, waiting for transfers between devices, per_device(): full_panels = lax.all_gather(panels, 'fsdp', axis=0, tiled=True)  79.9 us
    unnamed x60, local copies, waits for them, and re-layouts  20.7 us
  transfers between devices with their start and end apart: 5, of which 3 were waited for; matrix products, arithmetic and copies ran while one was open for 6% of the time, Pallas kernels for 0%

commit v1 on v0

--- a/solution.py
+++ b/solution.py
@@ -152,7 +152,7 @@
         flat_tokens, d_all, (((0,), (0,)), ((), ())), preferred_element_type=jnp.float32
     )
     reduced = lax.psum_scatter(grads, "fsdp", scatter_dimension=0, tiled=True)
-    summed = lax.psum(reduced, ("dp", "ctx"))
+    summed = lax.psum(lax.psum(reduced, "ctx"), "dp")
     return (
         dechunked,
         grad_tokens,

time: 864 us -> 764 us (0.88)
  waiting for transfers between devices: 588 us -> 487 us
    psum x1 -> x2, waiting for transfers between devices: 362 us -> 261 us  [per_device(): summed = lax.psum(lax.psum(reduced, 'ctx'), 'dp')]
  transfers between devices with their start and end apart: 5 -> 6, of which waited for: 3 -> 4; matrix products, arithmetic and copies ran while one was open for 6% -> 6% of each run, Pallas kernels for 0% -> 0%
where the time goes in v1:
time: 764 us; the launch traced here: 755 us
  waiting for transfers between devices  487 us (64%)
  blocking collectives  92 us (12%)
  local copies, waits for them, and re-layouts  58.6 us (8%)
  matrix products  50.1 us (7%)
  other arithmetic  46.9 us (6%)
  between operations  14.5 us (2%)
    psum x2, waiting for transfers between devices, per_device(): summed = lax.psum(lax.psum(reduced, 'ctx'), 'dp')  261 us
    reduce_scatter x1, waiting for transfers between devices, per_device(): reduced = lax.psum_scatter(grads, 'fsdp', scatter_dimension=0, tiled=True)  146 us
    all_gather x3, blocking collectives, carried_in(): gathered = jax.tree.map(lambda a: lax.all_gather(a, axis), part)  92 us
    all_gather x1, waiting for transfers between devices, per_device(): full_panels = lax.all_gather(panels, 'fsdp', axis=0, tiled=True)  79.9 us
    unnamed x60, local copies, waits for them, and re-layouts  20.7 us
    dot_general x1, matrix products, per_device(): lax.dot_general(flat_tokens, d_all, (((0,), (0,)), ((), ())), preferred_e...  15.4 us
  transfers between devices with their start and end apart: 6, of which 4 were waited for; matrix products, arithmetic and copies ran while one was open for 6% of the time, Pallas kernels for 0%

profile of v1, /device:TPU:0, one launch (start us, length us, event | category | flops | bytes accessed | tf_op | source)
XLA Modules:
  0.0 755.4 jit_solution(17243269309327315147)
XLA Ops:
  7.2 3.2 pad_maximum_fusion.2
  10.5 2.0 copy.154
  13.1 79.9 %all-gather.4.cloned.1.call-done = bf16[1024,4096]{1,0:T(8,128)(2,1)} async-done(((bf16[256,4096]{1,0:T(8,128)(2,1)}), bf16[1024,4096]{1,0:T(8,128)(2,1)}) %all-gather.4.cloned.1.call-update) | async-done | bytes 8388624 | tf_op jit(solution)/shard_map/all_gather | solution.py:47
  93.1 6.9 convolution_bitcast_fusion.1
  100.7 4.6 collective-permute-start
  105.6 2.9 copy.153
  109.4 0.6 multiply_multiply_fusion.1
  110.2 0.8 copy.129
  111.0 1.2 reduce_window_sum.26
  112.9 0.6 copy-done.16
  113.6 7.8 %fusion.21 = f32[1,4,128,16,128]{4,2,3,1,0:T(8,128)S(1)} fusion(f32[4,128,16,128]{3,2,1,0:T(8,128)} %bitcast.152, f32[4,16,128]{2,1,0:T(8,128)S(1)} %get-tuple-element.516, f32[4,16,128]{2,1,0:T(8,128)S(1)} %copy.130, pred[128,128]{1,0:T(8,128)(4,1)S(1)} %iota_compare_fusion.1), kind=kOutput, calls=%fused_computation.38 | convolution fusion | flops 1614807040 | bytes 8470528 | tf_op jit(solution)/shard_map/bnhtu,bnuhc->bnthc/dot_general | solution.py:75
  121.4 1.9 copy-done.6
  123.4 2.9 while.58
  123.4 0.6 fusion.66
  124.8 0.7 fusion.66
  125.6 0.7 fusion.66
  126.3 34.6 %all-gather = f32[8,16,128]{2,1,0:T(8,128)S(1)} all-gather(f32[1,16,128]{2,1,0:T(8,128)S(1)} %get-tuple-element.266), channel_id=2, replica_groups=mesh['dp'=4,'fsdp'=4,'ctx'=8] {'ctx'}, dimensions={0}, use_global_device_ids=true | all-gather | bytes 73728 | tf_op jit(solution)/shard_map/all_gather | solution.py:20
  161.0 0.7 reduce_window_sum.28
  162.2 22.3 %all_gather.22 = f32[8,1,16]{2,1,0:T(1,128)} all-gather(f32[1,1,16]{2,1,0:T(1,128)S(1)} %get-tuple-element.521), channel_id=1, replica_groups=mesh['dp'=4,'fsdp'=4,'ctx'=8] {'ctx'}, dimensions={0}, use_global_device_ids=true | all-gather | bytes 576 | tf_op jit(solution)/shard_map/all_gather | solution.py:20
  184.5 1.5 fusion.50
  186.1 1.3 fusion.53
  187.4 5.0 fusion.18
  192.4 2.0 copy-done.7
  194.6 2.9 while.59
  194.6 0.7 fusion.67
  195.3 0.7 fusion.67
  196.8 0.6 fusion.67
  197.5 35.0 %all-gather.1 = f32[8,16,128]{2,1,0:T(8,128)S(1)} all-gather(f32[1,16,128]{2,1,0:T(8,128)S(1)} %get-tuple-element.269), channel_id=3, replica_groups=mesh['dp'=4,'fsdp'=4,'ctx'=8] {'ctx'}, dimensions={0}, use_global_device_ids=true | all-gather | bytes 73728 | tf_op jit(solution)/shard_map/all_gather | solution.py:20
  232.5 5.4 while.57
  232.5 0.6 dynamic-slice_bitcast_fusion.5
  233.2 0.7 dynamic-slice_bitcast_fusion.5
  235.3 0.6 dynamic-slice_bitcast_fusion.5
  236.0 0.7 dynamic-slice_bitcast_fusion.5
  238.0 0.8 bitcast_add_fusion.4
  238.8 3.8 fusion.59
  242.6 2.4 copy.143
  245.1 2.2 slice.76
  247.4 2.6 pad_maximum_fusion.1
  250.0 0.8 copy-done.3
  250.9 1.3 copy-done.8
  252.2 3.8 fusion.16
  256.2 2.1 multiply_bitcast_fusion
  258.3 1.0 copy-done.9
  259.2 1.3 collective-permute-start.1
  260.5 4.4 copy.146
  265.0 2.8 mul.510
  267.8 9.8 %multiply_convert_fusion = bf16[1,512,2048]{2,0,1:T(2,128)(2,1)} fusion(f32[1,512,2048]{2,0,1:T(1,128)} %bitcast.151, f32[1,512,2048]{2,0,1:T(1,128)} %bitcast.150), kind=kLoop, calls=%fused_computation.34 | loop fusion | flops 2097152 | bytes 10485760 | tf_op jit(solution)/shard_map/convert_element_type | solution.py:125
  277.6 2.2 fusion.47
  280.1 1.6 copy.147
  281.8 1.6 copy.148
  283.4 9.9 %pad_maximum_fusion = bf16[1,512,4096]{2,0,1:T(2,128)(2,1)S(1)} fusion(bf16[1,512,2048]{2,0,1:T(2,128)(2,1)S(1)} %copy-done.2, bf16[1,512,1024]{2,0,1:T(2,128)(2,1)S(1)} %copy.148, bf16[1,512,1024]{2,0,1:T(2,128)(2,1)S(1)} %copy.147), kind=kLoop, calls=%fused_computation.13 | loop fusion | flops 12582912 | bytes 8388608 | tf_op jit(solution)/shard_map/concatenate | solution.py:144
  293.3 3.2 copy-done.5
  296.6 15.4 %convolution_bitcast_fusion = f32[1024,4096]{0,1:T(8,128)} fusion(bf16[1,512,4096]{2,0,1:T(2,128)(2,1)S(1)} %pad_maximum_fusion, bf16[1,512,1024]{2,1,0:T(8,128)(2,1)S(1)} %copy-done), kind=kOutput, calls=%fused_computation.12 | convolution fusion | flops 4294967296 | bytes 22020096 | tf_op jit(solution)/shard_map/dot_general | solution.py:151
  312.1 146.3 %reduce-scatter.2.cloned.1.call-done = f32[256,4096]{0,1:T(8,128)} async-done(((f32[1024,4096]{0,1:T(8,128)}), f32[256,4096]{0,1:T(8,128)}) %reduce-scatter.2.cloned.1.call-update) | async-done | bytes 4194320 | tf_op jit(solution)/shard_map/reduce_scatter | solution.py:154
  458.4 188.7 %all-reduce.3.cloned.1.call-done = f32[256,4096]{0,1:T(8,128)} async-done(((f32[256,4096]{0,1:T(8,128)}), f32[256,4096]{0,1:T(8,128)}) %all-reduce.3.cloned.1.call-update) | async-done | bytes 4194320 | tf_op jit(solution)/shard_map/psum | solution.py:155
  647.1 2.7 copy.137
  649.8 4.4 convert_element_type.52
  654.2 14.9 %fusion.44 = bf16[1,512,1024]{2,1,0:T(8,128)(2,1)} fusion(bf16[1024,4096]{1,0:T(8,128)(2,1)} %all-gather.4.cloned.1.call-done, bf16[1,512,4096]{2,0,1:T(2,128)(2,1)} %copy-done.5), kind=kOutput, calls=%fused_computation.64 | convolution fusion | flops 4295491584 | bytes 13631488 | tf_op jit(solution)/shard_map/dot_general | solution.py:147
  669.1 71.8 %all-reduce.5.cloned.1.call-done = f32[256,4096]{0,1:T(8,128)} async-done(((f32[256,4096]{0,1:T(8,128)}), f32[256,4096]{0,1:T(8,128)}) %all-reduce.5.cloned.1.call-update) | async-done | bytes 4194320 | tf_op jit(solution)/shard_map/psum | solution.py:155
  740.9 1.6 slice-done
  742.5 1.8 copy.151
  744.3 1.7 fusion.60
  746.0 1.3 copy.149
  747.3 1.3 copy.150
  (118 shorter events, 9.4 us)
Async XLA Ops:
  7.2 85.9 %copy-start = (bf16[1,512,1024]{2,1,0:T(8,128)(2,1)S(1)}, bf16[1,512,1024]{2,1,0:T(8,128)(2,1)}, u32[]{:S(2)}) copy-start(bf16[1,512,1024]{2,1,0:T(8,128)(2,1)} %param.15) | copy-start | bytes 3145732
  7.2 3.4 copy-start.11
  7.2 85.9 %all-gather.4.cloned.1.call-start = ((), (), s32[]{:S(2)}) async-start(), calls=%async_computation.1 | async-start | bytes 10485760 | tf_op jit(solution)/shard_map/all_gather | solution.py:47
  10.5 447.9 %reduce-scatter.2.cloned.1.call-start = ((), (), s32[]{:S(2)}) async-start(), calls=%async_computation.2 | async-start | bytes 20971520 | tf_op jit(solution)/shard_map/reduce_scatter | solution.py:154
  100.0 8.6 %copy-start.1 = (f32[512,4096]{1,0:T(8,128)}, f32[512,4096]{1,0:T(8,128)S(1)}, u32[]{:S(2)}) copy-start(f32[512,4096]{1,0:T(8,128)S(1)} %convolution_bitcast_fusion.1) | copy-start | bytes 25165828
  100.7 7.8 %collective-permute-start = (f32[1,1,1024]{2,1,0:T(1,128)S(1)}, f32[1,1,1024]{2,1,0:T(1,128)S(1)}, u32[]{:S(2)}, u32[]{:S(2)}) collective-permute-start(f32[1,1,1024]{2,1,0:T(1,128)S(1)} %slice.70), channel_id=1, source_target_pairs={{0,1},{1,2},{2,3},{3,4},{4,5},{5,6},{6,7},{8,9},{9,10},{10,11},{11... | collective-permute-start | bytes 12296 | tf_op jit(solution)/shard_map/ppermute | solution.py:13
  108.5 1.6 copy-start.23
  108.5 1.6 copy-start.25
  108.5 1.6 copy-start.14
  110.1 2.8 copy-start.18
  112.9 0.6 copy-start.16
  121.4 1.9 copy-start.6
  161.7 22.8 %copy-start.22 = (f32[1,4,16]{2,1,0:T(4,128)}, f32[1,4,16]{2,1,0:T(4,128)S(1)}, u32[]{:S(2)}) copy-start(f32[1,4,16]{2,1,0:T(4,128)S(1)} %reduce_window_sum.28) | copy-start | bytes 772
  187.4 50.5 %copy-start.13 = (f32[4,128,16]{2,1,0:T(8,128)S(1)}, f32[4,128,16]{2,1,0:T(8,128)}, u32[]{:S(2)}) copy-start(f32[4,128,16]{2,1,0:T(8,128)} %get-tuple-element.508) | copy-start | bytes 98308
  192.4 2.0 copy-start.7
  245.1 2.2 copy-start.12
  247.4 3.5 copy-start.3
  247.4 4.7 copy-start.8
  252.1 3.9 copy-start.26
  252.1 4.0 copy-start.24
  252.1 4.0 copy-start.15
  252.1 4.0 copy-start.17
  252.1 4.0 copy-start.21
  258.3 1.0 copy-start.9
  259.2 22.5 %collective-permute-start.1 = (bf16[1,1,1024]{2,1,0:T(2,128)(2,1)S(1)}, bf16[1,1,1024]{2,1,0:T(2,128)(2,1)S(1)}, u32[]{:S(2)}, u32[]{:S(2)}) collective-permute-start(bf16[1,1,1024]{2,1,0:T(2,128)(2,1)S(1)} %slice.78), channel_id=1, source_target_pairs={{1,0},{2,1},{3,2},{4,3},{5,4},{6,5},{7,6},{9,8},{10,9},{11,10},{12... | collective-permute-start | bytes 6152 | tf_op jit(solution)/shard_map/ppermute | solution.py:13
  260.5 4.4 copy-start.19
  267.8 9.8 %copy-start.20 = (f32[512]{0:T(512)S(1)}, f32[512]{0:T(512)}, u32[]{:S(2)}) copy-start(f32[512]{0:T(512)} %get-tuple-element.511) | copy-start | bytes 6148
  277.6 2.2 copy-start.10
  280.0 3.4 copy-start.2
  293.3 3.2 copy-start.5
  312.0 335.1 %all-reduce.3.cloned.1.call-start = ((), (), s32[]{:S(2)}) async-start(), calls=%async_computation.3 | async-start | bytes 8388608 | tf_op jit(solution)/shard_map/psum | solution.py:155
  458.3 188.8 %copy-start.4 = (bf16[1,4,128,16,128]{4,2,3,1,0:T(8,128)(2,1)S(1)}, bf16[1,4,128,16,128]{4,2,3,1,0:T(8,128)(2,1)}, u32[]{:S(2)}) copy-start(bf16[1,4,128,16,128]{4,2,3,1,0:T(8,128)(2,1)} %get-tuple-element.501) | copy-start | bytes 6291460
  458.4 282.6 %all-reduce.5.cloned.1.call-start = ((), (), s32[]{:S(2)}) async-start(), calls=%async_computation.4 | async-start | bytes 8388608 | tf_op jit(solution)/shard_map/psum | solution.py:155
  740.9 1.6 slice-start
Sparse Core Ops, SparseCore 0:
  10.6 82.4 all-gather.3
  312.1 146.1 reduce-scatter.1
  460.9 186.1 all-reduce.2
  649.3 91.5 all-reduce.4
